TPU v7x, 32 devices: a whole 2x2x4 slice. The times are simulated.
32 devices in a mesh: dp: 4 (over y, x), mp: 8 (over z, core).
Axes of the slice: x: 2, y: 2, z: 4, core: 2. Of those that a mesh axis runs over, the one named last changes fastest.
Arguments:
- tokens: bfloat16 [1024, 8192], P('dp', 'mp'), may hold values from -6 to 6
- base_weight: bfloat16 [24576, 8192], P('mp'), may hold values from -0.0625 to 0.0625
- block_values: bfloat16 [256, 128, 128], P('mp'), may hold values from -0.0625 to 0.0625
- block_ids: int32 [2, 256], P(None, 'mp'), may hold values from -1 to 63, as said below
- lowrank_model: float32 [8192, 256], P('mp'), may hold values from -6 to 6
- lowrank_hidden: float32 [24576, 256], P('mp'), may hold values from -6 to 6
- output_cotangent: bfloat16 [1024, 24576], P('dp', 'mp'), may hold values from -6 to 6
Outputs:
- projection_output: bfloat16 [1024, 24576], P('dp', 'mp')
- input_cotangent: bfloat16 [1024, 8192], P('dp', 'mp')
- block_grads: float32 [256, 128, 128], P(('mp', 'dp'))
- updated_model: float32 [8192, 256], P('mp')
- updated_hidden: float32 [24576, 256], P('mp')
Inputs may be any that keep to these rules, and one draw needn't show every extreme that they name: `block_ids`: slots 32 * m to 32 * (m + 1) - 1 belong to index m of mp. A live slot has row 0 in 0 to 23 and row 1 in 0 to 63; the live slots of one index come first and name distinct blocks; the remaining slots hold -1 in both rows. Every index has 8 or more live slots, and some index has all 32.
All inputs are finite; a program needn't handle non-finite values.
Results may differ from a plain program's by a relative error of at most 0.0065.
Values may be sent and summed in bfloat16 or wider, within the bound.
A program may use at most 384 MiB of HBM per device.

v0:
```python
import math
import jax
import jax.numpy as jnp
from jax import lax
from jax.sharding import PartitionSpec as P


def partner_2(value, axis, distance):
    return lax.ppermute(value, axis, [(i, i ^ 1 << distance) for i in range(lax.axis_size(axis))])


def shards(
    tokens, base_weight, block_values, block_ids, lowrank_model, lowrank_hidden, output_cotangent
):
    tok_rows = tokens.shape[0]
    mp_size = lax.axis_size("mp")
    dp_size = lax.axis_size("dp")
    total_tokens = tok_rows * dp_size
    f_local = base_weight.shape[0]
    feature_width = base_weight.shape[1]
    hidden_total = f_local * mp_size
    nb_local = block_values.shape[0]
    block_size = block_values.shape[1]
    adapter_factor_rank = lowrank_model.shape[1]
    col_blocks = feature_width // block_size
    row_blocks = f_local // block_size
    adapter_scale = 0.5 / math.sqrt(adapter_factor_rank * feature_width)
    row_ids = block_ids[0]
    col_ids = block_ids[1]
    live_slots = row_ids >= 0
    flat_index = jnp.where(live_slots, row_ids * col_blocks + col_ids, -1)
    placer = (
        flat_index[:, None] == jnp.arange(row_blocks * col_blocks, dtype=jnp.int32)[None, :]
    ).astype(jnp.bfloat16)
    dense_blocks = lax.dot_general(
        placer,
        block_values.reshape(nb_local, block_size * block_size),
        (((0,), (0,)), ((), ())),
        preferred_element_type=jnp.float32,
    )
    dense_blocks = (
        dense_blocks.reshape(row_blocks, col_blocks, block_size, block_size)
        .transpose(0, 2, 1, 3)
        .reshape(f_local, feature_width)
    )
    effective = (base_weight.astype(jnp.float32) + dense_blocks).astype(jnp.bfloat16)
    gathered = lax.all_gather(tokens, "mp", axis=1, tiled=True)
    model_half = lowrank_model.astype(jnp.bfloat16)
    hidden_half = lowrank_hidden.astype(jnp.bfloat16)
    v_partial = jnp.dot(output_cotangent, hidden_half, preferred_element_type=jnp.float32)
    model_rows = lax.all_gather(model_half, "mp", axis=0, tiled=True)
    u_summed = jnp.dot(gathered, model_rows, preferred_element_type=jnp.float32)
    v_summed = lax.psum(v_partial, "mp")
    left_factor_shard = u_summed.astype(jnp.bfloat16)
    right_factor_shard = v_summed.astype(jnp.bfloat16)
    base_projection_output = lax.dot_general(
        gathered, effective, (((1,), (1,)), ((), ())), preferred_element_type=jnp.float32
    )
    lowrank_output = lax.dot_general(
        left_factor_shard, hidden_half, (((1,), (1,)), ((), ())), preferred_element_type=jnp.float32
    )
    projection_output = (base_projection_output + adapter_scale * lowrank_output).astype(
        jnp.bfloat16
    )
    backward_lowrank_term = lax.dot_general(
        right_factor_shard, model_half, (((1,), (1,)), ((), ())), preferred_element_type=jnp.float32
    )
    backward_base_term = lax.psum_scatter(
        lax.dot_general(
            effective,
            output_cotangent,
            (((0,), (1,)), ((), ())),
            preferred_element_type=jnp.float32,
        ),
        "mp",
        scatter_dimension=0,
        tiled=True,
    ).T
    input_cotangent = (backward_base_term + adapter_scale * backward_lowrank_term).astype(
        jnp.bfloat16
    )
    right_factor_gradient_part = adapter_scale * lax.dot_general(
        output_cotangent,
        left_factor_shard,
        (((0,), (0,)), ((), ())),
        preferred_element_type=jnp.float32,
    )
    left_factor_gradient_part = adapter_scale * lax.dot_general(
        tokens, right_factor_shard, (((0,), (0,)), ((), ())), preferred_element_type=jnp.float32
    )
    hidden_side_gradient, model_side_gradient = (
        lax.psum(right_factor_gradient_part.astype(jnp.bfloat16), "dp").astype(jnp.float32),
        lax.psum(left_factor_gradient_part.astype(jnp.bfloat16), "dp").astype(jnp.float32),
    )
    safe_rows = jnp.maximum(row_ids, 0)
    safe_cols = jnp.maximum(col_ids, 0)
    grad_sel = jnp.take(
        output_cotangent.reshape(tok_rows, row_blocks, block_size), safe_rows, axis=1
    )
    token_sel = jnp.take(gathered.reshape(tok_rows, col_blocks, block_size), safe_cols, axis=1)
    block_part = jnp.einsum("tbi,tbj->bij", grad_sel, token_sel, preferred_element_type=jnp.float32)
    block_part = (
        block_part * (live_slots.astype(jnp.float32) / math.sqrt(total_tokens))[:, None, None]
    )
    block_grads = lax.psum_scatter(block_part, "dp", scatter_dimension=0, tiled=True)
    model_step = (
        lowrank_model
        - math.sqrt(adapter_factor_rank * feature_width / (total_tokens * hidden_total))
        * model_side_gradient
    )
    moved_hidden = (
        lowrank_hidden - math.sqrt(adapter_factor_rank / total_tokens) * hidden_side_gradient
    )
    gram_local = lax.dot_general(
        moved_hidden, moved_hidden, (((0,), (0,)), ((), ())), precision=lax.Precision.HIGHEST
    )
    lower_factor = jnp.linalg.cholesky(gram_local)
    levels = mp_size.bit_length() - 1
    for bit_index in range(levels):
        partner = partner_2(lower_factor.astype(jnp.bfloat16), "mp", bit_index).astype(
            lower_factor.dtype
        )
        own_gram = jnp.dot(lower_factor, lower_factor.T, precision=lax.Precision.HIGHEST)
        partner_gram = jnp.dot(partner, partner.T, precision=lax.Precision.HIGHEST)
        lower_factor = jnp.linalg.cholesky(own_gram + partner_gram)
    solved = lax.linalg.triangular_solve(
        lower_factor, moved_hidden, left_side=False, lower=True, transpose_a=True
    )
    updated_hidden = math.sqrt(hidden_total) * solved
    updated_model = jnp.dot(model_step, lower_factor, precision=lax.Precision.HIGHEST) / math.sqrt(
        hidden_total
    )
    return (projection_output, input_cotangent, block_grads, updated_model, updated_hidden)


def solution(mesh):
    in_specs = (
        P("dp", "mp"),
        P("mp", None),
        P("mp", None, None),
        P(None, "mp"),
        P("mp", None),
        P("mp", None),
        P("dp", "mp"),
    )
    out_specs = (
        P("dp", "mp"),
        P("dp", "mp"),
        P(("mp", "dp"), None, None),
        P("mp", None),
        P("mp", None),
    )
    return jax.shard_map(shards, mesh=mesh, in_specs=in_specs, out_specs=out_specs, check_vma=False)
```

profile of v0, /device:TPU:0, one launch (start us, length us, event | category | flops | bytes accessed | tf_op | source)
XLA Modules:
  0.0 534.8 jit_solution(5461947114065312162)
XLA Ops:
  7.2 2.2 copy.48
  9.5 2.1 convert_element_type.59
  11.6 2.0 fusion.29
  14.3 39.6 %all-reduce.6 = bf16[256,256]{1,0:T(8,128)(2,1)S(1)} all-reduce(f32[256,256]{1,0:T(8,128)S(1)} %fusion.29), channel_id=1, replica_groups=mesh['dp'=4,'mp'=8] {'mp'}, use_global_device_ids=true, to_apply=%region_1.2 | all-reduce | flops 65536 | bytes 393216 | tf_op jit(solution)/shard_map/psum | solution.py:53
  53.9 2.2 fusion.22
  56.1 37.0 %fusion.23 = f32[24,64,128,128]{3,1,2,0:T(8,128)} fusion(s32[24,64]{1,0:T(8,128)S(1)} %multiply_add_fusion, s32[32]{0:T(128)S(1)} %get-tuple-element.61, bf16[4,8,128,128]{3,2,1,0:T(8,128)(2,1)} %bitcast.154), kind=kOutput, calls=%fused_computation.40 | convolution fusion | flops 1610661888 | bytes 101718144 | tf_op jit(solution)/shard_map/dot_general | solution.py:35
  93.1 19.2 %all-gather.5.cloned.1.call-done = bf16[8192,256]{1,0:T(8,128)(2,1)} async-done(((bf16[1024,256]{1,0:T(8,128)(2,1)}), bf16[8192,256]{1,0:T(8,128)(2,1)}) %all-gather.5.cloned.1.call-update) | async-done | bytes 4194320 | tf_op jit(solution)/shard_map/all_gather | solution.py:51
  112.3 4.9 convolution_convert_fusion
  117.2 1.9 fusion.4
  119.4 56.7 %fusion.106 = f32[8192,256]{1,0:T(8,128)} fusion(bf16[256,3072]{1,0:T(8,128)(2,1)} %param.14, f32[384,8,64,128]{3,2,1,0:T(8,128)} %bitcast.42, bf16[3072,8192]{1,0:T(8,128)(2,1)} %param.9), kind=kOutput, calls=%fused_computation.165 | convolution fusion | flops 12960399360 | bytes 160956416 | tf_op jit(solution)/shard_map/dot_general | solution.py:69
  176.1 2.6 copy.51
  178.8 2.6 copy.52
  181.4 3.6 gather_fusion
  185.0 91.2 %convolution_bitcast_fusion = f32[256,3072]{0,1:T(8,128)} fusion(bf16[256,8192]{0,1:T(8,128)(2,1)} %all-gather.3.cloned.1.call-done, f32[384,8,64,128]{3,2,1,0:T(8,128)} %bitcast.42, bf16[3072,8192]{1,0:T(8,128)(2,1)} %param.9), kind=kOutput, calls=%fused_computation.6 | convolution fusion | flops 12960399360 | bytes 158334976 | tf_op jit(solution)/shard_map/dot_general | solution.py:56
  276.2 3.7 fusion.2
  279.9 2.6 copy.67
  282.4 6.8 %copy.53 = bf16[256,64,128]{2,0,1:T(8,128)(2,1)} copy(bf16[256,64,128]{0,2,1:T(8,128)(2,1)} %bitcast.152) | data formatting | bytes 8388608 | tf_op jit(solution)/shard_map/reshape | solution.py:100
  289.3 4.5 gather_fusion.1
  293.8 3.9 fusion.14
  297.7 2.7 multiply_subtract_fusion
  300.4 5.1 fusion.110
  308.1 11.7 %cholesky.214 = f32[128,128]{1,0:T(8,128)S(1)} custom-call(f32[128,128]{1,0:T(8,128)S(1)} %cholesky.346), custom_call_target="Cholesky" | custom-call | tf_op jit(solution)/shard_map/jit(cholesky)/cholesky | solution.py:117
  319.8 10.0 %custom-call.15 = f32[1,128,128]{1,2,0:T(8,128)S(1)} custom-call(f32[1,128,128]{2,1,0:T(8,128)S(1)} %get-tuple-element.56), custom_call_target="InvertDiagBlocksLowerTriangular" | custom-call | tf_op jit(solution)/shard_map/jit(cholesky)/cholesky | solution.py:117
  330.8 1.1 convolution_subtract_fusion.1
  332.0 11.7 %cholesky.231 = f32[128,128]{1,0:T(8,128)S(1)} custom-call(f32[128,128]{1,0:T(8,128)S(1)} %convolution_subtract_fusion.1), custom_call_target="Cholesky" | custom-call | tf_op jit(solution)/shard_map/jit(cholesky)/cholesky | solution.py:117
  350.0 11.7 %cholesky.248 = f32[128,128]{1,0:T(8,128)S(1)} custom-call(f32[128,128]{1,0:T(8,128)S(1)} %cholesky.349), custom_call_target="Cholesky" | custom-call | tf_op jit(solution)/shard_map/jit(cholesky)/cholesky | solution.py:125
  361.7 9.8 %custom-call.16 = f32[1,128,128]{1,2,0:T(8,128)S(1)} custom-call(f32[1,128,128]{2,1,0:T(8,128)S(1)} %get-tuple-element.52), custom_call_target="InvertDiagBlocksLowerTriangular" | custom-call | tf_op jit(solution)/shard_map/jit(cholesky)/cholesky | solution.py:125
  372.6 1.1 slice_subtract_fusion.2
  373.7 11.9 %cholesky.265 = f32[128,128]{1,0:T(8,128)S(1)} custom-call(f32[128,128]{1,0:T(8,128)S(1)} %slice_subtract_fusion.2), custom_call_target="Cholesky" | custom-call | tf_op jit(solution)/shard_map/jit(cholesky)/cholesky | solution.py:125
  389.3 4.8 collective-permute-done.1
  396.8 11.7 %cholesky.282 = f32[128,128]{1,0:T(8,128)S(1)} custom-call(f32[128,128]{1,0:T(8,128)S(1)} %cholesky.352), custom_call_target="Cholesky" | custom-call | tf_op jit(solution)/shard_map/jit(cholesky)/cholesky | solution.py:125
  408.6 9.8 %custom-call.17 = f32[1,128,128]{1,2,0:T(8,128)S(1)} custom-call(f32[1,128,128]{2,1,0:T(8,128)S(1)} %get-tuple-element.48), custom_call_target="InvertDiagBlocksLowerTriangular" | custom-call | tf_op jit(solution)/shard_map/jit(cholesky)/cholesky | solution.py:125
  420.6 12.1 %cholesky.299 = f32[128,128]{1,0:T(8,128)S(1)} custom-call(f32[128,128]{1,0:T(8,128)S(1)} %slice_subtract_fusion.1), custom_call_target="Cholesky" | custom-call | tf_op jit(solution)/shard_map/jit(cholesky)/cholesky | solution.py:125
  435.3 1.4 collective-permute-start.2
  437.2 6.5 %collective-permute-done.2 = bf16[256,256]{1,0:T(8,128)(2,1)S(1)} collective-permute-done((bf16[256,256]{1,0:T(8,128)(2,1)S(1)}, bf16[256,256]{1,0:T(8,128)(2,1)S(1)}, u32[]{:S(2)}, u32[]{:S(2)}) %collective-permute-start.2) | collective-permute-done | bytes 131104 | tf_op jit(solution)/shard_map/ppermute | solution.py:9
  446.4 11.7 %cholesky.316 = f32[128,128]{1,0:T(8,128)S(1)} custom-call(f32[128,128]{1,0:T(8,128)S(1)} %cholesky.355), custom_call_target="Cholesky" | custom-call | tf_op jit(solution)/shard_map/jit(cholesky)/cholesky | solution.py:125
  458.2 9.8 %custom-call.18 = f32[1,128,128]{1,2,0:T(8,128)S(1)} custom-call(f32[1,128,128]{2,1,0:T(8,128)S(1)} %get-tuple-element.44), custom_call_target="InvertDiagBlocksLowerTriangular" | custom-call | tf_op jit(solution)/shard_map/jit(cholesky)/cholesky | solution.py:125
  470.2 11.9 %cholesky.333 = f32[128,128]{1,0:T(8,128)S(1)} custom-call(f32[128,128]{1,0:T(8,128)S(1)} %slice_subtract_fusion), custom_call_target="Cholesky" | custom-call | tf_op jit(solution)/shard_map/jit(cholesky)/cholesky | solution.py:125
  485.4 6.8 %while.1 = (s32[]{:T(128)}, f32[256,256]{1,0:T(8,128)}, s32[2,2]{1,0:T(2,128)S(1)}, f32[2,128,128]{2,1,0:T(8,128)}, s32[]{:T(128)}) while((s32[]{:T(128)}, f32[256,256]{1,0:T(8,128)}, s32[2,2]{1,0:T(2,128)S(1)}, f32[2,128,128]{2,1,0:T(8,128)}, s32[]{:T(128)}) %tuple.44), condition=%wide.while_cond, body=%wide.while_body.sunk | while | flops 2 | bytes 132205 | solution.py:126
  486.0 2.8 bitcast_dynamic-update-slice_fusion.2
  489.5 2.8 bitcast_dynamic-update-slice_fusion.2
  492.2 20.5 %custom-call.11 = f32[2,128,128]{1,2,0:T(8,128)S(1)} custom-call(f32[2,128,128]{2,1,0:T(8,128)} %get-tuple-element.13), custom_call_target="InvertDiagBlocksLowerTriangular" | custom-call | tf_op jit(solution)/shard_map/triangular_solve | solution.py:126
  512.7 1.6 fusion.12
  514.3 3.5 convolution_subtract_fusion
  517.8 1.6 fusion.66
  519.7 2.4 copy.69
  522.1 3.4 convolution_multiply_fusion.4
  525.5 1.6 fusion.20
  (106 shorter events, 29.4 us)
Async XLA Ops:
  7.2 4.5 copy-start
  7.2 85.9 %all-gather.3.cloned.1.call-start = ((), (), s32[]{:S(2)}) async-start(), calls=%async_computation.2 | async-start | bytes 4718592 | tf_op jit(solution)/shard_map/all_gather | solution.py:47
  9.4 102.9 %all-gather.5.cloned.1.call-start = ((), (), s32[]{:S(2)}) async-start(), calls=%async_computation.3 | async-start | bytes 4718592 | tf_op jit(solution)/shard_map/all_gather | solution.py:51
  11.6 2.1 copy-start.10
  11.6 286.1 %all-reduce.5.cloned.1.call-start = ((), (), s32[]{:S(2)}) async-start(), calls=%async_computation.6 | async-start | bytes 4194304 | tf_op jit(solution)/shard_map/psum | solution.py:93
  53.9 39.2 %copy-start.4 = (bf16[256,256]{1,0:T(8,128)(2,1)}, bf16[256,256]{1,0:T(8,128)(2,1)S(1)}, u32[]{:S(2)}) copy-start(bf16[256,256]{1,0:T(8,128)(2,1)S(1)} %all-reduce.6) | copy-start | bytes 393220
  112.3 4.9 copy-start.1
  119.2 406.3 %reduce-scatter.3.cloned.1.call-start = ((), (), s32[]{:S(2)}) async-start(), calls=%async_computation.4 | async-start | bytes 9437184 | tf_op jit(solution)/shard_map/reduce_scatter | solution.py:68
  176.1 5.3 copy-start.12
  176.1 5.3 copy-start.13
  176.1 351.9 %reduce-scatter.5.cloned.1.call-start = ((), (), s32[]{:S(2)}) async-start(), calls=%async_computation.5 | async-start | bytes 2621440 | tf_op jit(solution)/shard_map/reduce_scatter | solution.py:105
  178.8 6.2 %copy-start.11 = (s32[2,32]{1,0:T(2,128)S(1)}, s32[2,32]{1,0:T(2,128)}, u32[]{:S(2)}) copy-start(s32[2,32]{1,0:T(2,128)} %param.11) | copy-start | bytes 772
  289.3 4.5 copy-start.3
  307.3 0.7 copy-start.7
  345.7 1.5 collective-permute-start
  349.2 0.7 copy-start.8
  388.2 5.8 %collective-permute-start.1 = (bf16[256,256]{1,0:T(8,128)(2,1)S(1)}, bf16[256,256]{1,0:T(8,128)(2,1)S(1)}, u32[]{:S(2)}, u32[]{:S(2)}) collective-permute-start(bf16[256,256]{1,0:T(8,128)(2,1)S(1)} %fusion.46), channel_id=1, source_target_pairs={{0,2},{1,3},{2,0},{3,1},{4,6},{5,7},{6,4},{7,5},{8,10},{9,11},{10,... | collective-permute-start | bytes 393224 | tf_op jit(solution)/shard_map/ppermute | solution.py:9
  396.1 0.7 copy-start.9
  435.3 8.3 %collective-permute-start.2 = (bf16[256,256]{1,0:T(8,128)(2,1)S(1)}, bf16[256,256]{1,0:T(8,128)(2,1)S(1)}, u32[]{:S(2)}, u32[]{:S(2)}) collective-permute-start(bf16[256,256]{1,0:T(8,128)(2,1)S(1)} %fusion.43), channel_id=1, source_target_pairs={{0,4},{1,5},{2,6},{3,7},{4,0},{5,1},{6,2},{7,3},{8,12},{9,13},{10,... | collective-permute-start | bytes 393224 | tf_op jit(solution)/shard_map/ppermute | solution.py:9
  445.7 0.7 copy-start.6
  519.7 5.8 %copy-start.5 = (bf16[256,256]{1,0:T(8,128)(2,1)S(1)}, bf16[256,256]{1,0:T(8,128)(2,1)}, u32[]{:S(2)}) copy-start(bf16[256,256]{1,0:T(8,128)(2,1)} %copy-done.4) | copy-start | bytes 393220
  522.1 3.4 copy-start.2
Sparse Core Ops, SparseCore 0:
  10.2 53.7 all-gather.2
  66.2 46.1 all-gather.4
  119.3 68.2 all-reduce.4
  189.8 89.5 reduce-scatter.2
  297.8 34.5 reduce-scatter.4
where the time goes:
time: 541 us; the launch traced here: 535 us
  matrix products  231 us (43%)
  other arithmetic  169 us (31%)
  local copies, waits for them, and re-layouts  41.4 us (8%)
  blocking collectives  39.6 us (7%)
  waiting for transfers between devices  31.2 us (6%)
  between operations  19.6 us (4%)
    another operation x21, other arithmetic, shards(): lower_factor = jnp.linalg.cholesky(own_gram + partner_gram)  104 us
    dot_general x1, matrix products, shards(): lax.dot_general(gathered, effective, (((1,), (1,)), ((), ())), preferred_...  91.2 us
    dot_general x1, matrix products, shards(): lax.dot_general(effective, output_cotangent, (((0,), (1,)), ((), ())), pr...  56.7 us
    psum x1, blocking collectives, shards(): v_summed = lax.psum(v_partial, 'mp')  39.6 us
    dot_general x1, matrix products, shards(): lax.dot_general(placer, block_values.reshape(nb_local, block_size * block...  37 us
    another operation x6, other arithmetic, shards(): lower_factor = jnp.linalg.cholesky(gram_local)  34.1 us
    another operation x3, other arithmetic, shards(): lax.linalg.triangular_solve(lower_factor, moved_hidden, left_side=False,...  21.2 us
    all_gather x1, waiting for transfers between devices, shards(): model_rows = lax.all_gather(model_half, 'mp', axis=0, tiled=True)  19.2 us
  transfers between devices with their start and end apart: 8, of which 4 were waited for; matrix products, arithmetic and copies ran while one was open for 80% of the time, Pallas kernels for 0%

commit v1 on v0

--- a/solution.py
+++ b/solution.py
@@ -50,7 +50,7 @@
     v_partial = jnp.dot(output_cotangent, hidden_half, preferred_element_type=jnp.float32)
     model_rows = lax.all_gather(model_half, "mp", axis=0, tiled=True)
     u_summed = jnp.dot(gathered, model_rows, preferred_element_type=jnp.float32)
-    v_summed = lax.psum(v_partial, "mp")
+    v_summed = jnp.sum(lax.all_gather(v_partial, axis_name="mp"), axis=0)
     left_factor_shard = u_summed.astype(jnp.bfloat16)
     right_factor_shard = v_summed.astype(jnp.bfloat16)
     base_projection_output = lax.dot_general(

time: 541 us -> 663 us (1.23)
  matrix products: 231 us -> 301 us
  waiting for transfers between devices: 31.2 us -> 100 us
  blocking collectives: 39.6 us -> 0 us
  other arithmetic: 169 us -> 194 us
    dot_general x1, matrix products: 56.7 us -> 124 us  [shards(): lax.dot_general(effective, output_cotangent, (((0,), (1,)), ((), ())), pr...]
    all_gather x1, waiting for transfers between devices: 0.01 us -> 40.1 us  [shards(): gathered = lax.all_gather(tokens, 'mp', axis=1, tiled=True)]
    psum x1 -> x0, blocking collectives: 39.6 us -> none  [shards(): v_summed = lax.psum(v_partial, 'mp')]
    all_gather x1, waiting for transfers between devices: 19.2 us -> 47.9 us  [shards(): model_rows = lax.all_gather(model_half, 'mp', axis=0, tiled=True)]
    another operation x21, other arithmetic: 104 us -> 122 us  [shards(): lower_factor = jnp.linalg.cholesky(own_gram + partner_gram)]
    unnamed x33 -> x31, local copies, waits for them, and re-layouts: 13.6 us -> 10.5 us
  transfers between devices with their start and end apart: 8 -> 9, of which waited for: 4 -> 5; matrix products, arithmetic and copies ran while one was open for 80% -> 79% of each run, Pallas kernels for 0% -> 0%
where the time goes in v1:
time: 663 us; the launch traced here: 656 us
  matrix products  301 us (45%)
  other arithmetic  194 us (29%)
  waiting for transfers between devices  100 us (15%)
  local copies, waits for them, and re-layouts  38.1 us (6%)
  between operations  20.2 us (3%)
    dot_general x1, matrix products, shards(): lax.dot_general(effective, output_cotangent, (((0,), (1,)), ((), ())), pr...  124 us
    another operation x21, other arithmetic, shards(): lower_factor = jnp.linalg.cholesky(own_gram + partner_gram)  122 us
    dot_general x1, matrix products, shards(): lax.dot_general(gathered, effective, (((1,), (1,)), ((), ())), preferred_...  92.1 us
    all_gather x1, waiting for transfers between devices, shards(): model_rows = lax.all_gather(model_half, 'mp', axis=0, tiled=True)  47.9 us
    another operation x6, other arithmetic, shards(): lower_factor = jnp.linalg.cholesky(gram_local)  40.2 us
    all_gather x1, waiting for transfers between devices, shards(): gathered = lax.all_gather(tokens, 'mp', axis=1, tiled=True)  40.1 us
    dot_general x1, matrix products, shards(): lax.dot_general(placer, block_values.reshape(nb_local, block_size * block...  35.4 us
    another operation x3, other arithmetic, shards(): lax.linalg.triangular_solve(lower_factor, moved_hidden, left_side=False,...  21.8 us
  transfers between devices with their start and end apart: 9, of which 5 were waited for; matrix products, arithmetic and copies ran while one was open for 79% of the time, Pallas kernels for 0%

profile of v1, /device:TPU:0, one launch (start us, length us, event | category | flops | bytes accessed | tf_op | source)
XLA Modules:
  0.0 655.8 jit_solution(8657644360949495767)
XLA Ops:
  7.2 3.7 fusion.29
  13.1 35.4 %fusion.23 = f32[24,64,128,128]{3,1,2,0:T(8,128)} fusion(s32[24,64]{1,0:T(8,128)S(1)} %multiply_add_fusion, s32[32]{0:T(128)S(1)} %get-tuple-element.61, bf16[4,8,128,128]{3,2,1,0:T(8,128)(2,1)S(1)} %bitcast.156), kind=kOutput, calls=%fused_computation.40 | convolution fusion | flops 1610661888 | bytes 101718144 | tf_op jit(solution)/shard_map/dot_general | solution.py:35
  48.5 1.7 reduce_sum.9
  51.4 40.1 %all-gather.5.cloned.1.call-done = bf16[256,8192]{0,1:T(8,128)(2,1)} async-done(((bf16[256,1024]{0,1:T(8,128)(2,1)}), bf16[256,8192]{0,1:T(8,128)(2,1)}) %all-gather.5.cloned.1.call-update) | async-done | bytes 4194320 | tf_op jit(solution)/shard_map/all_gather | solution.py:47
  91.5 47.9 %all-gather.7.cloned.1.call-done = bf16[8192,256]{1,0:T(8,128)(2,1)} async-done(((bf16[1024,256]{1,0:T(8,128)(2,1)}), bf16[8192,256]{1,0:T(8,128)(2,1)}) %all-gather.7.cloned.1.call-update) | async-done | bytes 4194320 | tf_op jit(solution)/shard_map/all_gather | solution.py:51
  139.4 4.8 convolution_convert_fusion
  144.2 1.9 fusion.4
  146.2 124.0 %fusion.106 = f32[8192,256]{1,0:T(8,128)} fusion(bf16[256,3072]{1,0:T(8,128)(2,1)S(1)} %copy-done.1, f32[384,8,64,128]{3,2,1,0:T(8,128)} %bitcast.43, bf16[3072,8192]{1,0:T(8,128)(2,1)} %param.9), kind=kOutput, calls=%fused_computation.165 | convolution fusion | flops 12960399360 | bytes 160956416 | tf_op jit(solution)/shard_map/dot_general | solution.py:69
  271.9 2.2 gather_fusion
  274.1 92.1 %convolution_bitcast_fusion = f32[256,3072]{0,1:T(8,128)} fusion(bf16[256,8192]{0,1:T(8,128)(2,1)} %all-gather.5.cloned.1.call-done, f32[384,8,64,128]{3,2,1,0:T(8,128)} %bitcast.43, bf16[3072,8192]{1,0:T(8,128)(2,1)} %param.9), kind=kOutput, calls=%fused_computation.6 | convolution fusion | flops 12960399360 | bytes 158334976 | tf_op jit(solution)/shard_map/dot_general | solution.py:56
  366.2 3.7 fusion.2
  369.9 2.6 copy.67
  372.5 6.4 copy.53
  378.8 4.5 gather_fusion.1
  383.3 3.9 fusion.14
  387.3 2.7 multiply_subtract_fusion
  389.9 5.1 fusion.110
  397.6 12.3 %cholesky.214 = f32[128,128]{1,0:T(8,128)} custom-call(f32[128,128]{1,0:T(8,128)S(1)} %cholesky.346), custom_call_target="Cholesky" | custom-call | tf_op jit(solution)/shard_map/jit(cholesky)/cholesky | solution.py:117
  412.3 11.7 %custom-call.15 = f32[1,128,128]{1,2,0:T(8,128)} custom-call(f32[1,128,128]{2,1,0:T(8,128)} %get-tuple-element.56), custom_call_target="InvertDiagBlocksLowerTriangular" | custom-call | tf_op jit(solution)/shard_map/jit(cholesky)/cholesky | solution.py:117
  425.1 1.7 convolution_subtract_fusion.1
  426.8 13.2 %cholesky.231 = f32[128,128]{1,0:T(8,128)} custom-call(f32[128,128]{1,0:T(8,128)} %convolution_subtract_fusion.1), custom_call_target="Cholesky" | custom-call | tf_op jit(solution)/shard_map/jit(cholesky)/cholesky | solution.py:117
  447.0 12.3 %cholesky.248 = f32[128,128]{1,0:T(8,128)} custom-call(f32[128,128]{1,0:T(8,128)S(1)} %cholesky.349), custom_call_target="Cholesky" | custom-call | tf_op jit(solution)/shard_map/jit(cholesky)/cholesky | solution.py:125
  460.2 1.5 fusion.88
  461.7 11.3 %custom-call.16 = f32[1,128,128]{1,2,0:T(8,128)} custom-call(f32[1,128,128]{2,1,0:T(8,128)} %get-tuple-element.52), custom_call_target="InvertDiagBlocksLowerTriangular" | custom-call | tf_op jit(solution)/shard_map/jit(cholesky)/cholesky | solution.py:125
  474.1 1.7 slice_subtract_fusion.2
  475.8 13.3 %cholesky.265 = f32[128,128]{1,0:T(8,128)} custom-call(f32[128,128]{1,0:T(8,128)} %slice_subtract_fusion.2), custom_call_target="Cholesky" | custom-call | tf_op jit(solution)/shard_map/jit(cholesky)/cholesky | solution.py:125
  493.4 5.0 collective-permute-done.1
  501.2 12.3 %cholesky.282 = f32[128,128]{1,0:T(8,128)} custom-call(f32[128,128]{1,0:T(8,128)S(1)} %cholesky.352), custom_call_target="Cholesky" | custom-call | tf_op jit(solution)/shard_map/jit(cholesky)/cholesky | solution.py:125
  514.4 1.5 fusion.86
  515.9 11.3 %custom-call.17 = f32[1,128,128]{1,2,0:T(8,128)} custom-call(f32[1,128,128]{2,1,0:T(8,128)} %get-tuple-element.48), custom_call_target="InvertDiagBlocksLowerTriangular" | custom-call | tf_op jit(solution)/shard_map/jit(cholesky)/cholesky | solution.py:125
  528.2 1.7 slice_subtract_fusion.1
  530.0 13.4 %cholesky.299 = f32[128,128]{1,0:T(8,128)} custom-call(f32[128,128]{1,0:T(8,128)} %slice_subtract_fusion.1), custom_call_target="Cholesky" | custom-call | tf_op jit(solution)/shard_map/jit(cholesky)/cholesky | solution.py:125
  548.6 6.6 %collective-permute-done.2 = bf16[256,256]{1,0:T(8,128)(2,1)S(1)} collective-permute-done((bf16[256,256]{1,0:T(8,128)(2,1)S(1)}, bf16[256,256]{1,0:T(8,128)(2,1)S(1)}, u32[]{:S(2)}, u32[]{:S(2)}) %collective-permute-start.2) | collective-permute-done | bytes 131104 | tf_op jit(solution)/shard_map/ppermute | solution.py:9
  557.9 12.3 %cholesky.316 = f32[128,128]{1,0:T(8,128)} custom-call(f32[128,128]{1,0:T(8,128)S(1)} %cholesky.355), custom_call_target="Cholesky" | custom-call | tf_op jit(solution)/shard_map/jit(cholesky)/cholesky | solution.py:125
  571.1 1.5 select_reduce_fusion.1
  572.6 11.3 %custom-call.18 = f32[1,128,128]{1,2,0:T(8,128)} custom-call(f32[1,128,128]{2,1,0:T(8,128)} %get-tuple-element.44), custom_call_target="InvertDiagBlocksLowerTriangular" | custom-call | tf_op jit(solution)/shard_map/jit(cholesky)/cholesky | solution.py:125
  585.0 1.7 slice_subtract_fusion
  586.7 13.4 %cholesky.333 = f32[128,128]{1,0:T(8,128)} custom-call(f32[128,128]{1,0:T(8,128)} %slice_subtract_fusion), custom_call_target="Cholesky" | custom-call | tf_op jit(solution)/shard_map/jit(cholesky)/cholesky | solution.py:125
  604.4 6.8 %while.1 = (s32[]{:T(128)}, f32[256,256]{1,0:T(8,128)}, s32[2,2]{1,0:T(2,128)S(1)}, f32[2,128,128]{2,1,0:T(8,128)}, s32[]{:T(128)}) while((s32[]{:T(128)}, f32[256,256]{1,0:T(8,128)}, s32[2,2]{1,0:T(2,128)S(1)}, f32[2,128,128]{2,1,0:T(8,128)}, s32[]{:T(128)}) %tuple.44), condition=%wide.while_cond, body=%wide.while_body.sunk | while | flops 2 | bytes 132205 | solution.py:126
  605.0 2.8 bitcast_dynamic-update-slice_fusion.2
  608.4 2.8 bitcast_dynamic-update-slice_fusion.2
  611.2 21.1 %custom-call.11 = f32[2,128,128]{1,2,0:T(8,128)} custom-call(f32[2,128,128]{2,1,0:T(8,128)} %get-tuple-element.13), custom_call_target="InvertDiagBlocksLowerTriangular" | custom-call | tf_op jit(solution)/shard_map/triangular_solve | solution.py:126
  632.3 2.4 fusion.12
  634.7 3.5 convolution_subtract_fusion
  638.3 1.6 fusion.66
  640.2 2.4 copy.69
  642.5 3.4 convolution_multiply_fusion.4
  646.0 1.6 fusion.20
  (107 shorter events, 40.2 us)
Async XLA Ops:
  7.2 3.9 copy-start.5
  7.2 5.0 copy-start.3
  7.2 41.3 %all-gather.9.cloned.1.call-start = ((), (), s32[]{:S(2)}) async-start(), calls=%async_computation.6 | async-start | bytes 2359296 | tf_op jit(solution)/shard_map/all_gather | solution.py:53
  11.0 2.1 copy-start.12
  11.0 2.1 copy-start.6
  11.0 80.5 %all-gather.5.cloned.1.call-start = ((), (), s32[]{:S(2)}) async-start(), calls=%async_computation.2 | async-start | bytes 4718592 | tf_op jit(solution)/shard_map/all_gather | solution.py:47
  12.1 127.3 %all-gather.7.cloned.1.call-start = ((), (), s32[]{:S(2)}) async-start(), calls=%async_computation.3 | async-start | bytes 4718592 | tf_op jit(solution)/shard_map/all_gather | solution.py:51
  13.0 374.2 %all-reduce.4.cloned.1.call-start = ((), (), s32[]{:S(2)}) async-start(), calls=%async_computation.7 | async-start | bytes 4194304 | tf_op jit(solution)/shard_map/psum | solution.py:93
  51.4 92.8 %copy-start.1 = (bf16[256,3072]{1,0:T(8,128)(2,1)S(1)}, bf16[256,3072]{1,0:T(8,128)(2,1)}, u32[]{:S(2)}) copy-start(bf16[256,3072]{1,0:T(8,128)(2,1)} %param.14) | copy-start | bytes 4718596
  146.1 499.8 %reduce-scatter.3.cloned.1.call-start = ((), (), s32[]{:S(2)}) async-start(), calls=%async_computation.4 | async-start | bytes 9437184 | tf_op jit(solution)/shard_map/reduce_scatter | solution.py:68
  270.2 378.3 %reduce-scatter.5.cloned.1.call-start = ((), (), s32[]{:S(2)}) async-start(), calls=%async_computation.5 | async-start | bytes 2621440 | tf_op jit(solution)/shard_map/reduce_scatter | solution.py:105
  274.1 92.1 %copy-start = (f32[3072,256]{1,0:T(8,128)S(1)}, f32[3072,256]{1,0:T(8,128)}, u32[]{:S(2)}) copy-start(f32[3072,256]{1,0:T(8,128)} %param.13) | copy-start | bytes 9437188
  378.8 4.5 copy-start.4
  396.9 0.7 copy-start.8
  442.9 1.4 collective-permute-start
  446.3 0.7 copy-start.9
  492.6 5.8 collective-permute-start.1
  500.5 0.7 copy-start.10
  546.8 8.3 %collective-permute-start.2 = (bf16[256,256]{1,0:T(8,128)(2,1)S(1)}, bf16[256,256]{1,0:T(8,128)(2,1)S(1)}, u32[]{:S(2)}, u32[]{:S(2)}) collective-permute-start(bf16[256,256]{1,0:T(8,128)(2,1)S(1)} %fusion.43), channel_id=1, source_target_pairs={{0,4},{1,5},{2,6},{3,7},{4,0},{5,1},{6,2},{7,3},{8,12},{9,13},{10,... | collective-permute-start | bytes 393224 | tf_op jit(solution)/shard_map/ppermute | solution.py:9
  557.2 0.7 copy-start.7
  634.7 3.6 copy-start.11
  642.5 3.4 copy-start.2
Sparse Core Ops, SparseCore 0:
  11.1 31.8 all-gather.8
  45.2 46.2 all-gather.4
  93.7 45.6 all-gather.6
  146.2 68.2 all-reduce.3
  270.3 88.2 reduce-scatter.2
  387.4 34.0 reduce-scatter.4
